TPU v7x, 32 devices: a whole 2x2x4 slice. The times are simulated.
32 devices in a mesh: dp: 4 (over y, x), context: 8 (over z, core).
Axes of the slice: x: 2, y: 2, z: 4, core: 2. Of those that a mesh axis runs over, the one named last changes fastest.
Arguments:
- projected: bfloat16 [4096, 6144], P(('dp', 'context')), may hold values from -6 to 6
- short_taps: float32 [3, 6144], replicated, may hold values from -4 to 4
- long_filter: float32 [2048, 1024], P('context'), may hold values from -1.5 to 1.5
- skip_gain: float32 [2048], P('context'), may hold values from -4 to 4
- out_proj: bfloat16 [2048, 2048], P('dp'), may hold values from -0.125 to 0.125
- cotangent: bfloat16 [4096, 2048], P(('dp', 'context')), may hold values from -25 to 25
Outputs:
- grad_inputs: bfloat16 [4096, 6144], P(('dp', 'context'))
- grad_taps: float32 [3, 6144], replicated
- grad_filter: float32 [2048, 1024], P('context', 'dp')
- grad_skip: float32 [2048], P('context')
- grad_proj: float32 [2048, 2048], P(('dp', 'context'))
All inputs are finite; a program needn't handle non-finite values.
Results may differ from a plain program's by a relative error of at most 0.012.
Values may be sent and summed in bfloat16 or wider, within the bound.
No kernel may reach another device: no remote copies, remote signals or barrier semaphores. Data moves between devices by JAX's collectives and lax.ppermute only.
A program may use at most 128 MiB of HBM per device.

v0:
```python
import math
import jax
import jax.numpy as jnp
from jax import lax
from jax.sharding import PartitionSpec as P

PRECISE = lax.Precision.HIGH


def passed_along(value, axis, steps):
    count = lax.axis_size(axis)
    initial, last = (max(0, -steps), min(count, count - steps))
    return lax.ppermute(value, axis, [(source, source + steps) for source in range(initial, last)])


def angle_table(first_count, second_count, period):
    first_idx = lax.broadcasted_iota(jnp.int32, (first_count, second_count), 0)
    second_idx = lax.broadcasted_iota(jnp.int32, (first_count, second_count), 1)
    phases = first_idx * second_idx % period
    angles = phases.astype(jnp.float32) * (-2.0 * math.pi / period)
    return (jnp.cos(angles), jnp.sin(angles))


def make_tables(seq_len):
    radix_size = min(128, seq_len)
    blocks = 2 * seq_len // radix_size
    half_blocks = blocks // 2
    outer_re, outer_im = angle_table(blocks, blocks, blocks)
    twist = angle_table(blocks, radix_size, blocks * radix_size)
    inner_re, inner_im = angle_table(radix_size, radix_size, radix_size)
    first_table = jnp.concatenate([outer_re[:, :half_blocks], outer_im[:, :half_blocks]], 0)
    inner_fwd = jnp.concatenate(
        [jnp.concatenate([inner_re, inner_im], 1), jnp.concatenate([-inner_im, inner_re], 1)], 0
    )
    inner_back = jnp.concatenate(
        [jnp.concatenate([inner_re, -inner_im], 1), jnp.concatenate([inner_im, inner_re], 1)], 0
    )
    last_table = jnp.concatenate([outer_re[:half_blocks, :], outer_im[:half_blocks, :]], 1)
    return (first_table, twist, inner_fwd, inner_back, last_table)


def forward_spectrum(signal, tables):
    first_table, (twist_re, twist_im), inner_fwd, inner_back, last_table = tables
    blocks = twist_re.shape[0]
    radix_size = twist_re.shape[1]
    shaped = signal.reshape(signal.shape[0], blocks // 2, radix_size)
    first = jnp.einsum("kn,cnm->ckm", first_table, shaped, precision=PRECISE)
    first_re = first[:, :blocks]
    first_im = first[:, blocks:]
    turned = jnp.concatenate(
        [first_re * twist_re - first_im * twist_im, first_re * twist_im + first_im * twist_re], 2
    )
    return jnp.einsum("ckn,nm->ckm", turned, inner_fwd, precision=PRECISE)


def spectral_product(left, right, conjugate_left):
    width = left.shape[2] // 2
    left_re, left_im = (left[:, :, :width], left[:, :, width:])
    right_re, right_im = (right[:, :, :width], right[:, :, width:])
    if conjugate_left:
        return jnp.concatenate(
            [left_re * right_re + left_im * right_im, left_re * right_im - left_im * right_re], 2
        )
    return jnp.concatenate(
        [left_re * right_re - left_im * right_im, left_re * right_im + left_im * right_re], 2
    )


def inverse_real(spectrum, tables):
    first_table, (twist_re, twist_im), inner_fwd, inner_back, last_table = tables
    blocks = twist_re.shape[0]
    radix_size = twist_re.shape[1]
    undo = jnp.einsum("ckn,nm->ckm", spectrum, inner_back, precision=PRECISE)
    undo_re = undo[:, :, :radix_size]
    undo_im = undo[:, :, radix_size:]
    back = jnp.concatenate(
        [undo_re * twist_re + undo_im * twist_im, undo_im * twist_re - undo_re * twist_im], 1
    )
    result = jnp.einsum("nk,ckm->cnm", last_table, back, precision=PRECISE)
    return result.reshape(spectrum.shape[0], blocks // 2 * radix_size) / (blocks * radix_size)


def body(projected, short_taps, long_filter, skip_gain, out_proj, cotangent):
    tok_rows = projected.shape[0]
    chan_all = projected.shape[1] // 3
    prev_rows = passed_along(projected[tok_rows - 2 :], "context", 1)
    extended = jnp.concatenate([prev_rows, projected], 0).astype(jnp.float32)
    current = extended[2:]
    once_back = extended[1 : tok_rows + 1]
    twice_back = extended[:tok_rows]
    mixed = short_taps[0] * current + short_taps[1] * once_back + short_taps[2] * twice_back
    query = mixed[:, :chan_all].astype(jnp.bfloat16)
    keyed = mixed[:, chan_all : 2 * chan_all].astype(jnp.bfloat16)
    valued = mixed[:, 2 * chan_all :].astype(jnp.bfloat16)
    product = (keyed.astype(jnp.float32) * valued.astype(jnp.float32)).astype(jnp.bfloat16)
    product_chan = lax.all_to_all(product.T, "context", split_axis=0, concat_axis=1, tiled=True)
    seq_len = product_chan.shape[1]
    tables = make_tables(seq_len)
    prod_f = product_chan.astype(jnp.float32)
    filter_spec = forward_spectrum(long_filter, tables)
    prod_spec = forward_spectrum(prod_f, tables)
    long_chan = (
        inverse_real(spectral_product(filter_spec, prod_spec, False), tables)
        + skip_gain[:, None] * prod_f
    )
    long_tok = lax.all_to_all(
        long_chan.astype(jnp.bfloat16), "context", split_axis=1, concat_axis=0, tiled=True
    ).T
    gate = (query.astype(jnp.float32) * long_tok.astype(jnp.float32)).astype(jnp.bfloat16)
    grad_gate = lax.dot_general(
        cotangent,
        lax.all_gather(out_proj, "dp", axis=0, tiled=True),
        (((1,), (1,)), ((), ())),
        preferred_element_type=jnp.float32,
    ).astype(jnp.bfloat16)
    grad_rows = lax.psum_scatter(
        lax.dot_general(
            gate, cotangent, (((0,), (0,)), ((), ())), preferred_element_type=jnp.float32
        ),
        ("dp", "context"),
        scatter_dimension=0,
        tiled=True,
    )
    grad_query = grad_gate.astype(jnp.float32) * long_tok.astype(jnp.float32)
    grad_long = (grad_gate.astype(jnp.float32) * query.astype(jnp.float32)).astype(jnp.bfloat16)
    grad_chan = lax.all_to_all(
        grad_long.T, "context", split_axis=0, concat_axis=1, tiled=True
    ).astype(jnp.float32)
    grad_spec = forward_spectrum(grad_chan, tables)
    back_chan = (
        inverse_real(spectral_product(filter_spec, grad_spec, True), tables)
        + skip_gain[:, None] * grad_chan
    )
    filter_local = inverse_real(spectral_product(prod_spec, grad_spec, True), tables)
    grad_product = lax.all_to_all(
        back_chan.astype(jnp.bfloat16), "context", split_axis=1, concat_axis=0, tiled=True
    ).T
    scale_factor = 1.0 / math.sqrt(seq_len * lax.axis_size("dp"))
    grad_filter = (
        lax.psum_scatter(filter_local, "dp", scatter_dimension=1, tiled=True) * scale_factor
    )
    grad_skip = lax.psum(jnp.sum(grad_chan * prod_f, axis=1), "dp") * scale_factor
    grad_key = grad_product.astype(jnp.float32) * valued.astype(jnp.float32)
    grad_value = grad_product.astype(jnp.float32) * keyed.astype(jnp.float32)
    grad_mixed = jnp.concatenate([grad_query, grad_key, grad_value], 1)
    next_rows = passed_along(grad_mixed[:2].astype(jnp.bfloat16), "context", -1).astype(jnp.float32)
    grad_ext = jnp.concatenate([grad_mixed, next_rows], 0)
    grad_inputs = (
        short_taps[0] * grad_ext[:tok_rows]
        + short_taps[1] * grad_ext[1 : tok_rows + 1]
        + short_taps[2] * grad_ext[2:]
    ).astype(jnp.bfloat16)
    taps_terms = jnp.stack(
        [
            jnp.sum(grad_mixed * current, 0),
            jnp.sum(grad_mixed * once_back, 0),
            jnp.sum(grad_mixed * twice_back, 0),
        ]
    )
    grad_taps = lax.psum(taps_terms, ("dp", "context")) * scale_factor
    return (grad_inputs, grad_taps, grad_filter, grad_skip, grad_rows * scale_factor)


def solution(mesh):
    placed = (
        P(("dp", "context"), None),
        P(),
        P("context", None),
        P("context"),
        P("dp", None),
        P(("dp", "context"), None),
    )
    return jax.shard_map(
        body,
        mesh=mesh,
        in_specs=placed,
        out_specs=(
            P(("dp", "context"), None),
            P(),
            P("context", "dp"),
            P("context"),
            P(("dp", "context"), None),
        ),
        check_vma=False,
    )
```

profile of v0, /device:TPU:0, one launch (start us, length us, event | category | flops | bytes accessed | tf_op | source)
XLA Modules:
  0.0 625.5 jit_solution(3541810269681701199)
XLA Ops:
  7.2 0.7 all-gather.2.cloned.1.call-update
  7.9 0.9 slice.124
  8.8 2.4 collective-permute-start
  11.2 1.1 fusion.109
  12.9 1.7 copy-done.1
  14.6 1.0 add_convert_fusion
  15.6 84.6 %all-gather.2.cloned.1.call-done = bf16[2048,2048]{1,0:T(8,128)(2,1)} async-done(((bf16[512,2048]{1,0:T(8,128)(2,1)}), bf16[2048,2048]{1,0:T(8,128)(2,1)}) %all-gather.2.cloned.1.call-update) | async-done | bytes 8388624 | tf_op jit(solution)/shard_map/all_gather | solution.py:112
  100.2 6.2 fusion.21
  106.5 1.0 copy-done.11
  107.6 1.0 copy.71
  108.6 4.6 all-to-all-start.2
  113.4 1.4 copy.77
  115.5 3.9 convolution_bitcast_fusion.2
  119.5 9.1 %all-to-all-done.2 = bf16[8,256,128]{2,1,0:T(8,128)(2,1)S(1)} async-done(((bf16[8,256,128]{2,1,0:T(8,128)(2,1)}), bf16[8,256,128]{2,1,0:T(8,128)(2,1)S(1)}, u32[]{:S(2)}, u32[]{:S(2)}) %all-to-all-start.2) | async-done | bytes 524320 | tf_op jit(solution)/shard_map/all_to_all | solution.py:126
  128.6 1.4 convolution_bitcast_fusion
  130.0 1.0 copy-done.7
  131.0 0.9 multiply_subtract_fusion.8
  131.8 0.7 pad_maximum_fusion
  132.6 4.2 fusion.16
  136.8 4.2 fusion.12
  141.0 0.9 multiply_add_fusion.3
  142.0 1.0 copy-done.5
  143.0 2.6 pad_maximum_fusion.4
  145.5 5.5 copy.61
  151.0 4.0 fusion.68
  155.7 3.2 fusion.46
  159.0 17.8 %all_to_all.52 = bf16[256,8,128]{2,0,1:T(8,128)(2,1)S(1)} all-to-all(bf16[256,8,128]{2,0,1:T(8,128)(2,1)S(1)} %copy.52), channel_id=1, replica_groups=mesh['dp'=4,'context'=8] {'context'}, dimensions={1} | all-to-all | bytes 1048576 | tf_op jit(solution)/shard_map/all_to_all | solution.py:135
  176.9 1.3 copy.74
  178.2 2.8 convert_multiply_fusion.5
  181.2 17.8 %all_to_all.53 = bf16[8,256,128]{2,1,0:T(8,128)(2,1)S(1)} all-to-all(bf16[8,256,128]{2,1,0:T(8,128)(2,1)S(1)} %bitcast.96), channel_id=1, replica_groups=mesh['dp'=4,'context'=8] {'context'}, dimensions={0} | all-to-all | bytes 1048576 | tf_op jit(solution)/shard_map/all_to_all | solution.py:96
  199.0 0.8 copy-done.15
  199.8 1.4 convolution_bitcast_fusion.1
  202.0 4.1 fusion.14
  206.1 4.4 multiply_add_fusion.1
  210.5 4.6 pad_maximum_fusion.5
  215.1 5.5 copy.64
  220.6 6.1 fusion.66
  226.8 2.3 pad_maximum_fusion.2
  229.0 5.6 copy.58
  234.7 4.3 fusion.70
  239.0 2.8 multiply_add_fusion
  241.8 3.2 fusion.43
  245.1 17.8 %all_to_all.54 = bf16[256,8,128]{2,0,1:T(8,128)(2,1)S(1)} all-to-all(bf16[256,8,128]{2,0,1:T(8,128)(2,1)S(1)} %copy.43), channel_id=1, replica_groups=mesh['dp'=4,'context'=8] {'context'}, dimensions={1} | all-to-all | bytes 1048576 | tf_op jit(solution)/shard_map/all_to_all | solution.py:106
  262.9 1.1 convert_element_type.197
  263.9 2.6 copy.70
  266.5 1.7 bitcast_multiply_fusion
  268.4 1.3 collective-permute-start.1
  269.7 1.8 collective-permute-done.1
  271.9 1.6 copy-done.2
  273.5 3.0 multiply_reduce_fusion.2
  276.5 0.7 pad_maximum_fusion.12
  277.3 3.5 fusion.22
  280.8 1.2 copy.98
  282.0 9.1 %fusion.53 = f32[2048,2048]{1,0:T(8,128)} fusion(bf16[128,2048]{1,0:T(8,128)(2,1)S(1)} %copy-done, f32[2048,128]{0,1:T(8,128)S(1)} %copy-done.10, bf16[128,6144]{1,0:T(8,128)(2,1)} %copy-done.12), kind=kOutput, calls=%fused_computation.82 | convolution fusion | flops 1074528256 | bytes 18874368 | tf_op jit(solution)/shard_map/dot_general | solution.py:117
  291.2 1.0 copy-done.14
  292.4 1.1 fusion.52
  293.5 8.9 %psum.15 = f32[256]{0:T(256)S(1)} all-reduce(f32[256]{0:T(256)S(1)} %fusion.52), channel_id=1, replica_groups=mesh['dp'=4,'context'=8] {'dp'}, use_global_device_ids=true, to_apply=%region_6.7 | all-reduce | flops 256 | bytes 2048 | tf_op jit(solution)/shard_map/psum | solution.py:142
  302.4 0.6 broadcast_multiply_fusion.3
  303.0 93.5 %all-reduce.2.cloned.1.call-done = f32[3,6144]{1,0:T(4,128)} async-done(((f32[3,6144]{1,0:T(4,128)}), f32[3,6144]{1,0:T(4,128)}) %all-reduce.2.cloned.1.call-update) | async-done | bytes 73744 | tf_op jit(solution)/shard_map/psum | solution.py:160
  396.5 1.6 broadcast_multiply_fusion.2
  398.0 29.9 %reduce-scatter.3.cloned.1.call-done = f32[256,256]{1,0:T(8,128)} async-done(((f32[256,1024]{1,0:T(8,128)}), f32[256,256]{1,0:T(8,128)}) %reduce-scatter.3.cloned.1.call-update) | async-done | bytes 262160 | tf_op jit(solution)/shard_map/reduce_scatter | solution.py:140
  428.0 1.7 broadcast_multiply_fusion.1
  429.6 187.3 %reduce-scatter.5.cloned.1.call-done = f32[64,2048]{1,0:T(8,128)} async-done(((f32[2048,2048]{1,0:T(8,128)}), f32[64,2048]{1,0:T(8,128)}) %reduce-scatter.5.cloned.1.call-update) | async-done | bytes 524304 | tf_op jit(solution)/shard_map/reduce_scatter | solution.py:116
  616.9 1.9 broadcast_multiply_fusion
  (68 shorter events, 4.4 us)
Async XLA Ops:
  7.2 93.1 %copy-start = (bf16[128,2048]{1,0:T(8,128)(2,1)S(1)}, bf16[128,2048]{1,0:T(8,128)(2,1)}, u32[]{:S(2)}) copy-start(bf16[128,2048]{1,0:T(8,128)(2,1)} %param.11) | copy-start | bytes 1572868
  7.2 5.3 copy-start.20
  7.2 93.0 %all-gather.2.cloned.1.call-start = ((), (), s32[]{:S(2)}) async-start(), calls=%async_computation.6 | async-start | bytes 10485760 | tf_op jit(solution)/shard_map/all_gather | solution.py:112
  8.8 3.6 collective-permute-start
  12.9 1.7 copy-start.1
  15.6 90.9 %copy-start.12 = (bf16[128,6144]{1,0:T(8,128)(2,1)}, bf16[128,6144]{1,0:T(8,128)(2,1)S(1)}, u32[]{:S(2)}) copy-start(bf16[128,6144]{1,0:T(8,128)(2,1)S(1)} %add_convert_fusion) | copy-start | bytes 4718596
  106.5 1.0 copy-start.11
  108.6 20.0 %all-to-all-start.2 = ((bf16[8,256,128]{2,1,0:T(8,128)(2,1)}), bf16[8,256,128]{2,1,0:T(8,128)(2,1)S(1)}, u32[]{:S(2)}, u32[]{:S(2)}) async-start(bf16[8,256,128]{2,1,0:T(8,128)(2,1)} %bitcast.17), calls=%async_computation.2 | async-start | bytes 1048576 | tf_op jit(solution)/shard_map/all_to_all | solution.py:126
  113.2 283.3 %all-reduce.2.cloned.1.call-start = ((), (), s32[]{:S(2)}) async-start(), calls=%async_computation.7 | async-start | bytes 196608 | tf_op jit(solution)/shard_map/psum | solution.py:160
  128.6 26.9 %copy-start.13 = (bf16[8,256,128]{2,1,0:T(8,128)(2,1)}, bf16[8,256,128]{2,1,0:T(8,128)(2,1)S(1)}, u32[]{:S(2)}) copy-start(bf16[8,256,128]{2,1,0:T(8,128)(2,1)S(1)} %all-to-all-done.2) | copy-start | bytes 1572868
  128.6 2.4 copy-start.7
  136.8 4.2 copy-start.3
  141.0 1.9 copy-start.5
  155.1 0.7 copy-start.21
  199.0 0.8 copy-start.15
  201.9 4.1 copy-start.4
  202.0 4.1 copy-start.6
  220.6 6.1 copy-start.18
  220.6 6.1 copy-start.19
  234.7 4.3 copy-start.8
  239.0 2.8 copy-start.16
  262.9 5.3 copy-start.9
  268.4 3.1 collective-permute-start.1
  271.5 1.9 copy-start.2
  277.2 150.8 %reduce-scatter.3.cloned.1.call-start = ((), (), s32[]{:S(2)}) async-start(), calls=%async_computation.8 | async-start | bytes 1310720 | tf_op jit(solution)/shard_map/reduce_scatter | solution.py:140
  277.3 4.8 copy-start.10
  282.0 334.9 %reduce-scatter.5.cloned.1.call-start = ((), (), s32[]{:S(2)}) async-start(), calls=%async_computation.9 | async-start | bytes 17301504 | tf_op jit(solution)/shard_map/reduce_scatter | solution.py:116
  291.2 1.0 copy-start.14
  291.2 1.2 copy-start.17
Sparse Core Ops, SparseCore 0:
  9.9 90.2 all-gather.1
  277.3 119.1 all-reduce.1
  399.4 28.5 reduce-scatter.2
  430.2 186.6 reduce-scatter.4
where the time goes:
time: 631 us; the launch traced here: 626 us
  waiting for transfers between devices  407 us (65%)
  blocking collectives  62.2 us (10%)
  matrix products  58.9 us (9%)
  other arithmetic  39.3 us (6%)
  local copies, waits for them, and re-layouts  35.3 us (6%)
  between operations  14.5 us (2%)
  starting transfers between devices  8.42 us (1%)
    reduce_scatter x1, waiting for transfers between devices, body(): lax.psum_scatter(lax.dot_general(gate, cotangent, (((0,), (0,)), ((), ())...  187 us
    psum x1, waiting for transfers between devices, body(): grad_taps = lax.psum(taps_terms, ('dp', 'context')) * scale_factor  93.5 us
    all_gather x1, waiting for transfers between devices, body(): lax.all_gather(out_proj, 'dp', axis=0, tiled=True)  84.6 us
    reduce_scatter x1, waiting for transfers between devices, body(): lax.psum_scatter(filter_local, 'dp', scatter_dimension=1, tiled=True)  29.9 us
    all_to_all x1, blocking collectives, body(): lax.all_to_all(back_chan.astype(jnp.bfloat16), 'context', split_axis=1, c...  17.8 us
    all_to_all x1, blocking collectives, body(): lax.all_to_all(product.T, 'context', split_axis=0, concat_axis=1, tiled=T...  17.8 us
    all_to_all x1, blocking collectives, body(): lax.all_to_all(long_chan.astype(jnp.bfloat16), 'context', split_axis=1, c...  17.8 us
    dot_general x3, matrix products, inverse_real(): undo = jnp.einsum('ckn,nm->ckm', spectrum, inner_back, precision=PRECISE)  14.4 us
  transfers between devices with their start and end apart: 7, of which 6 were waited for; matrix products, arithmetic and copies ran while one was open for 5% of the time, Pallas kernels for 0%

commit v1 on v0

--- a/solution.py
+++ b/solution.py
@@ -3,8 +3,15 @@
 import jax.numpy as jnp
 from jax import lax
 from jax.sharding import PartitionSpec as P
+from jax.lax import psum
 
 PRECISE = lax.Precision.HIGH
+
+
+def finish_slot(unit, a_name, link_axis):
+    for rr in (a_name, link_axis):
+        unit = psum(unit, rr)
+    return unit
 
 
 def passed_along(value, axis, steps):
@@ -157,7 +164,7 @@
             jnp.sum(grad_mixed * twice_back, 0),
         ]
     )
-    grad_taps = lax.psum(taps_terms, ("dp", "context")) * scale_factor
+    grad_taps = finish_slot(taps_terms, a_name="context", link_axis="dp") * scale_factor
     return (grad_inputs, grad_taps, grad_filter, grad_skip, grad_rows * scale_factor)
 
 

time: 631 us -> 608 us (0.964)
  waiting for transfers between devices: 407 us -> 383 us
    psum x1 -> x2, waiting for transfers between devices: 93.5 us -> 70.2 us  [finish_slot(): unit = psum(unit, rr)]
  transfers between devices with their start and end apart: 7 -> 8, of which waited for: 6 -> 7; matrix products, arithmetic and copies ran while one was open for 5% -> 5% of each run, Pallas kernels for 0% -> 0%
where the time goes in v1:
time: 608 us; the launch traced here: 602 us
  waiting for transfers between devices  383 us (63%)
  blocking collectives  63.1 us (10%)
  matrix products  58.9 us (10%)
  other arithmetic  39.3 us (6%)
  local copies, waits for them, and re-layouts  35.3 us (6%)
  between operations  14.5 us (2%)
  starting transfers between devices  8.46 us (1%)
    reduce_scatter x1, waiting for transfers between devices, body(): lax.psum_scatter(lax.dot_general(gate, cotangent, (((0,), (0,)), ((), ())...  187 us
    all_gather x1, waiting for transfers between devices, body(): lax.all_gather(out_proj, 'dp', axis=0, tiled=True)  84.6 us
    psum x2, waiting for transfers between devices, finish_slot(): unit = psum(unit, rr)  70.2 us
    reduce_scatter x1, waiting for transfers between devices, body(): lax.psum_scatter(filter_local, 'dp', scatter_dimension=1, tiled=True)  28.9 us
    all_to_all x1, blocking collectives, body(): lax.all_to_all(back_chan.astype(jnp.bfloat16), 'context', split_axis=1, c...  17.8 us
    all_to_all x1, blocking collectives, body(): lax.all_to_all(product.T, 'context', split_axis=0, concat_axis=1, tiled=T...  17.8 us
    all_to_all x1, blocking collectives, body(): lax.all_to_all(long_chan.astype(jnp.bfloat16), 'context', split_axis=1, c...  17.8 us
    dot_general x3, matrix products, inverse_real(): undo = jnp.einsum('ckn,nm->ckm', spectrum, inner_back, precision=PRECISE)  14.4 us
  transfers between devices with their start and end apart: 8, of which 7 were waited for; matrix products, arithmetic and copies ran while one was open for 5% of the time, Pallas kernels for 0%

profile of v1, /device:TPU:0, one launch (start us, length us, event | category | flops | bytes accessed | tf_op | source)
XLA Modules:
  0.0 602.2 jit_solution(7970659599914391901)
XLA Ops:
  7.2 0.7 all-gather.2.cloned.1.call-update
  7.9 0.9 slice.124
  8.8 2.4 collective-permute-start
  11.2 1.1 fusion.109
  12.9 1.7 copy-done.1
  14.6 1.0 add_convert_fusion
  15.6 84.6 %all-gather.2.cloned.1.call-done = bf16[2048,2048]{1,0:T(8,128)(2,1)} async-done(((bf16[512,2048]{1,0:T(8,128)(2,1)}), bf16[2048,2048]{1,0:T(8,128)(2,1)}) %all-gather.2.cloned.1.call-update) | async-done | bytes 8388624 | tf_op jit(solution)/shard_map/all_gather | solution.py:119
  100.2 6.2 %fusion.21 = f32[128,2048]{1,0:T(8,128)S(1)} fusion(bf16[128,2048]{1,0:T(8,128)(2,1)S(1)} %copy-done, bf16[2048,2048]{1,0:T(8,128)(2,1)} %all-gather.2.cloned.1.call-done), kind=kOutput, calls=%fused_computation.36 | convolution fusion | flops 1074266112 | bytes 9961472 | tf_op jit(solution)/shard_map/dot_general | solution.py:117
  106.5 1.0 copy-done.11
  107.6 1.0 copy.71
  108.6 4.6 all-to-all-start.2
  113.4 1.4 copy.77
  115.5 3.9 convolution_bitcast_fusion.2
  119.5 9.1 %all-to-all-done.2 = bf16[8,256,128]{2,1,0:T(8,128)(2,1)S(1)} async-done(((bf16[8,256,128]{2,1,0:T(8,128)(2,1)}), bf16[8,256,128]{2,1,0:T(8,128)(2,1)S(1)}, u32[]{:S(2)}, u32[]{:S(2)}) %all-to-all-start.2) | async-done | bytes 524320 | tf_op jit(solution)/shard_map/all_to_all | solution.py:133
  128.6 1.4 convolution_bitcast_fusion
  130.0 1.0 copy-done.7
  131.0 0.9 multiply_subtract_fusion.8
  131.8 0.7 pad_maximum_fusion
  132.6 4.2 fusion.16
  136.8 4.2 fusion.12
  141.0 0.9 multiply_add_fusion.3
  142.0 1.0 copy-done.5
  143.0 2.6 pad_maximum_fusion.4
  145.5 5.5 copy.61
  151.0 4.0 fusion.68
  155.7 3.2 fusion.46
  159.0 17.8 %all_to_all.52 = bf16[256,8,128]{2,0,1:T(8,128)(2,1)S(1)} all-to-all(bf16[256,8,128]{2,0,1:T(8,128)(2,1)S(1)} %copy.52), channel_id=1, replica_groups=mesh['dp'=4,'context'=8] {'context'}, dimensions={1} | all-to-all | bytes 1048576 | tf_op jit(solution)/shard_map/all_to_all | solution.py:142
  176.9 1.3 copy.74
  178.2 2.8 convert_multiply_fusion.5
  181.2 17.8 %all_to_all.53 = bf16[8,256,128]{2,1,0:T(8,128)(2,1)S(1)} all-to-all(bf16[8,256,128]{2,1,0:T(8,128)(2,1)S(1)} %bitcast.96), channel_id=1, replica_groups=mesh['dp'=4,'context'=8] {'context'}, dimensions={0} | all-to-all | bytes 1048576 | tf_op jit(solution)/shard_map/all_to_all | solution.py:103
  199.0 0.8 copy-done.15
  199.8 1.4 convolution_bitcast_fusion.1
  202.0 4.1 fusion.14
  206.1 4.4 multiply_add_fusion.1
  210.5 4.6 pad_maximum_fusion.5
  215.1 5.5 copy.64
  220.6 6.1 %fusion.66 = f32[256,16,256]{2,1,0:T(8,128)} fusion(f32[256,16,256]{2,1,0:T(8,128)} %copy.64, f32[128,128]{0,1:T(8,128)S(1)} %get-tuple-element.42, f32[128,128]{0,1:T(8,128)S(1)} %get-tuple-element.41, f32[128,128]{0,1:T(8,128)S(1)} %fusion.83), kind=kOutput, calls=%fused_computation.99 | convolution fusion | flops 1610809344 | bytes 8585216 | tf_op jit(solution)/shard_map/ckn,nm->ckm/dot_general | solution.py:80
  226.8 2.3 pad_maximum_fusion.2
  229.0 5.6 copy.58
  234.7 4.3 fusion.70
  239.0 2.8 multiply_add_fusion
  241.8 3.2 fusion.43
  245.1 17.8 %all_to_all.54 = bf16[256,8,128]{2,0,1:T(8,128)(2,1)S(1)} all-to-all(bf16[256,8,128]{2,0,1:T(8,128)(2,1)S(1)} %copy.43), channel_id=1, replica_groups=mesh['dp'=4,'context'=8] {'context'}, dimensions={1} | all-to-all | bytes 1048576 | tf_op jit(solution)/shard_map/all_to_all | solution.py:113
  262.9 1.1 convert_element_type.197
  263.9 2.6 copy.70
  266.5 1.7 bitcast_multiply_fusion
  268.4 1.3 collective-permute-start.1
  269.7 1.8 collective-permute-done.1
  271.9 1.6 copy-done.2
  273.5 3.0 multiply_reduce_fusion.2
  276.5 0.7 pad_maximum_fusion.12
  277.3 50.4 %all-reduce.3.cloned.1.call-done = f32[3,6144]{1,0:T(4,128)} async-done(((f32[3,6144]{1,0:T(4,128)}), f32[3,6144]{1,0:T(4,128)}) %all-reduce.3.cloned.1.call-update) | async-done | bytes 73744 | tf_op jit(solution)/shard_map/psum | solution.py:13
  327.7 3.5 fusion.22
  331.2 1.2 copy.98
  332.5 9.1 %fusion.53 = f32[2048,2048]{1,0:T(8,128)} fusion(bf16[128,2048]{1,0:T(8,128)(2,1)S(1)} %copy-done, f32[2048,128]{0,1:T(8,128)S(1)} %copy-done.10, bf16[128,6144]{1,0:T(8,128)(2,1)} %copy-done.12), kind=kOutput, calls=%fused_computation.82 | convolution fusion | flops 1074528256 | bytes 18874368 | tf_op jit(solution)/shard_map/dot_general | solution.py:124
  341.7 1.0 copy-done.14
  342.8 1.1 fusion.52
  343.9 9.8 %psum.23 = f32[256]{0:T(256)S(1)} all-reduce(f32[256]{0:T(256)S(1)} %fusion.52), channel_id=1, replica_groups=mesh['dp'=4,'context'=8] {'dp'}, use_global_device_ids=true, to_apply=%region_7.8 | all-reduce | flops 256 | bytes 2048 | tf_op jit(solution)/shard_map/psum | solution.py:149
  354.3 19.8 %all-reduce.5.cloned.1.call-done = f32[3,6144]{1,0:T(4,128)} async-done(((f32[3,6144]{1,0:T(4,128)}), f32[3,6144]{1,0:T(4,128)}) %all-reduce.5.cloned.1.call-update) | async-done | bytes 73744 | tf_op jit(solution)/shard_map/psum | solution.py:13
  374.2 1.6 broadcast_multiply_fusion.2
  375.7 28.9 %reduce-scatter.3.cloned.1.call-done = f32[256,256]{1,0:T(8,128)} async-done(((f32[256,1024]{1,0:T(8,128)}), f32[256,256]{1,0:T(8,128)}) %reduce-scatter.3.cloned.1.call-update) | async-done | bytes 262160 | tf_op jit(solution)/shard_map/reduce_scatter | solution.py:147
  404.7 1.7 broadcast_multiply_fusion.1
  406.3 187.2 %reduce-scatter.5.cloned.1.call-done = f32[64,2048]{1,0:T(8,128)} async-done(((f32[2048,2048]{1,0:T(8,128)}), f32[64,2048]{1,0:T(8,128)}) %reduce-scatter.5.cloned.1.call-update) | async-done | bytes 524304 | tf_op jit(solution)/shard_map/reduce_scatter | solution.py:123
  593.6 1.9 broadcast_multiply_fusion
  (71 shorter events, 5.0 us)
Async XLA Ops:
  7.2 93.1 %copy-start = (bf16[128,2048]{1,0:T(8,128)(2,1)S(1)}, bf16[128,2048]{1,0:T(8,128)(2,1)}, u32[]{:S(2)}) copy-start(bf16[128,2048]{1,0:T(8,128)(2,1)} %param.11) | copy-start | bytes 1572868
  7.2 5.3 copy-start.20
  7.2 93.0 %all-gather.2.cloned.1.call-start = ((), (), s32[]{:S(2)}) async-start(), calls=%async_computation.6 | async-start | bytes 10485760 | tf_op jit(solution)/shard_map/all_gather | solution.py:119
  8.8 3.6 collective-permute-start
  12.9 1.7 copy-start.1
  15.6 90.9 %copy-start.12 = (bf16[128,6144]{1,0:T(8,128)(2,1)}, bf16[128,6144]{1,0:T(8,128)(2,1)S(1)}, u32[]{:S(2)}) copy-start(bf16[128,6144]{1,0:T(8,128)(2,1)S(1)} %add_convert_fusion) | copy-start | bytes 4718596
  106.5 1.0 copy-start.11
  108.6 20.0 %all-to-all-start.2 = ((bf16[8,256,128]{2,1,0:T(8,128)(2,1)}), bf16[8,256,128]{2,1,0:T(8,128)(2,1)S(1)}, u32[]{:S(2)}, u32[]{:S(2)}) async-start(bf16[8,256,128]{2,1,0:T(8,128)(2,1)} %bitcast.17), calls=%async_computation.2 | async-start | bytes 1048576 | tf_op jit(solution)/shard_map/all_to_all | solution.py:133
  113.2 214.4 %all-reduce.3.cloned.1.call-start = ((), (), s32[]{:S(2)}) async-start(), calls=%async_computation.7 | async-start | bytes 196608 | tf_op jit(solution)/shard_map/psum | solution.py:13
  128.6 26.9 %copy-start.13 = (bf16[8,256,128]{2,1,0:T(8,128)(2,1)}, bf16[8,256,128]{2,1,0:T(8,128)(2,1)S(1)}, u32[]{:S(2)}) copy-start(bf16[8,256,128]{2,1,0:T(8,128)(2,1)S(1)} %all-to-all-done.2) | copy-start | bytes 1572868
  128.6 2.4 copy-start.7
  136.8 4.2 copy-start.3
  141.0 1.9 copy-start.5
  155.1 0.7 copy-start.21
  199.0 0.8 copy-start.15
  201.9 4.1 copy-start.4
  202.0 4.1 copy-start.6
  220.6 6.1 %copy-start.18 = (f32[256,16,128]{0,2,1:T(8,128)S(1)}, f32[256,16,128]{0,2,1:T(8,128)}, u32[]{:S(2)}) copy-start(f32[256,16,128]{0,2,1:T(8,128)} %get-tuple-element.26) | copy-start | bytes 6291460
  220.6 6.1 %copy-start.19 = (f32[256,16,128]{0,2,1:T(8,128)S(1)}, f32[256,16,128]{0,2,1:T(8,128)}, u32[]{:S(2)}) copy-start(f32[256,16,128]{0,2,1:T(8,128)} %get-tuple-element.27) | copy-start | bytes 6291460
  234.7 4.3 copy-start.8
  239.0 2.8 copy-start.16
  262.9 5.3 copy-start.9
  268.4 3.1 collective-permute-start.1
  271.5 1.9 copy-start.2
  277.2 96.9 %all-reduce.5.cloned.1.call-start = ((), (), s32[]{:S(2)}) async-start(), calls=%async_computation.8 | async-start | bytes 196608 | tf_op jit(solution)/shard_map/psum | solution.py:13
  327.7 77.0 %reduce-scatter.3.cloned.1.call-start = ((), (), s32[]{:S(2)}) async-start(), calls=%async_computation.9 | async-start | bytes 1310720 | tf_op jit(solution)/shard_map/reduce_scatter | solution.py:147
  327.7 4.8 copy-start.10
  332.4 261.2 %reduce-scatter.5.cloned.1.call-start = ((), (), s32[]{:S(2)}) async-start(), calls=%async_computation.10 | async-start | bytes 17301504 | tf_op jit(solution)/shard_map/reduce_scatter | solution.py:123
  341.6 1.0 copy-start.14
  341.6 1.2 copy-start.17
Sparse Core Ops, SparseCore 0:
  9.9 90.2 all-gather.1
  277.3 50.2 all-reduce.2
  330.8 43.3 all-reduce.4
  376.9 27.7 reduce-scatter.2
  406.9 186.6 reduce-scatter.4
